TPU v7x, 32 devices: a whole 2x2x4 slice. The times are simulated.
32 devices in a mesh: gx: 8 (over y, x, core), gy: 4 (over z).
Axes of the slice: x: 2, y: 2, z: 4, core: 2. Of those that a mesh axis runs over, the one named last changes fastest.
Arguments:
- permeability: float32 [8192, 1024], P('gx', 'gy'), may hold values from 0.01 to 100
- basis: float32 [64, 8, 256, 256], P('gx', 'gy'), may hold values from 0 to 1, as said below
- support: int32 [64, 8, 256, 256], P('gx', 'gy'), may hold values from 0 to 1, as said below
Outputs:
- smoothed: float32 [64, 8, 256, 256], P('gx', 'gy')
Inputs may be any that keep to these rules, and one draw needn't show every extreme that they name: support is 1 exactly on a rectangle of the box that contains the block's own 128 x 128 cells in its middle and reaches 32 to 64 cells past them on each side, cut to the grid. basis is positive where support is 1 and 0 elsewhere.
All inputs are finite; a program needn't handle non-finite values.
Results may differ from a plain program's by a relative error of at most 0.0003.
Values sent between devices are 32-bit elements; how exact they have to be, the bound alone decides.
A program may use at most 128 MiB of HBM per device.

v0:
```python
import jax
import jax.numpy as jnp
from jax import lax
from jax.experimental import pallas as pl
from jax.experimental.pallas import tpu as pltpu
from jax.sharding import PartitionSpec as P

MESH = pl.DeviceIdType.MESH
relaxation = 2.0 / 3.0
coupling = relaxation / (1.0 - relaxation)
PAD = 8
CH = 16
NEAR = 40


def pick(k, table):
    value = jnp.int32(table[-1])
    for n in range(len(table) - 2, -1, -1):
        value = jnp.where(k == n, table[n], value)
    return value


def first_needs(order, count):
    seen, out = set(), []
    for rb in order:
        new = [q for q in (rb - 1, rb, rb + 1) if 0 <= q < count and q not in seen]
        seen.update(new)
        out.append(new)
    return out


def make_kernel(nx, ny, size_x, size_y, half):
    full = 2 * half
    last = nx
    strips = ny + 1
    hw = half // 2

    middle = list(range(3, nx - 2))
    pack_order = [1, nx - 1, 2, 0, nx, nx - 2] + middle
    weigh_order = [0, 1, nx, nx - 1, 2] + middle + [nx - 2]
    unpack_steps = first_needs(weigh_order, nx + 1)
    total_order = [1, nx - 1, 2, 3, 0, nx] + middle[1:] + [nx - 2]
    assert sorted(weigh_order) == sorted(pack_order) == sorted(total_order) == list(range(nx + 1))
    events, done, known = [], set(), set()
    for rb in total_order + [-1] * (nx + 1):
        known.add(rb)
        ready = [q for q in range(nx + 1) if q not in done and all(n in known for n in (q - 1, q, q + 1) if 0 <= n <= nx)]
        done.update(ready[:1])
        if rb >= 0 or ready:
            events.append((rb, ready[0] if ready else -1))
    assert len(done) == nx + 1
    resolve_order = [2, 3, 1, 0, nx] + [q for q in range(4, nx)]
    assert sorted(resolve_order) == list(range(nx + 1))
    resolve_steps = first_needs(resolve_order, nx + 1)

    def kernel(*refs):
        (perm_h, basis_h, out_h,
         a, b, d, w, s, lk, rz, rx, rec, got, px, pe, pk, pr, hk, hr,
         a_sem, p_sem, o_sem, zs_sem, zr_sem, xs_sem, xr_sem,
         ps_sem, pr_sem, hs_sem, hr_sem, rs_sem, rr_sem) = refs
        gx, gy = lax.axis_index("gx"), lax.axis_index("gy")
        has_up, has_down = gx > 0, gx < size_x - 1
        has_left, has_right = gy > 0, gy < size_y - 1
        up, down = (gx - 1, gy), (gx + 1, gy)
        left, right = (gx, gy - 1), (gx, gy + 1)
        z_sides = ((0, has_left, left), (1, has_right, right))
        x_sides = ((0, has_up, up), (1, has_down, down))
        halo = hw + PAD
        height = px.shape[0]
        length = height - 2 * halo

        def remote(src, dst, send, recv, target):
            return pltpu.make_async_remote_copy(
                src_ref=src, dst_ref=dst, send_sem=send, recv_sem=recv, device_id=target, device_id_type=MESH)

        def a_copy(i, h):
            return pltpu.make_async_copy(
                basis_h.at[i, :, :, pl.ds(h * half, half)], a.at[i + 1, :, h, pl.ds(PAD, full), :], a_sem.at[i, h])

        def o_copy(rb, part, h):
            lo = half if part == 0 else 0
            return pltpu.make_async_copy(
                d.at[rb + part, :, h, pl.ds(PAD + lo, half), :],
                out_h.at[rb - 1 + part, :, pl.ds(lo, half), pl.ds(h * half, half)], o_sem.at[rb, part, h])

        def row_copy(side, target):
            src, dst = (0, height - halo) if side == 0 else (length - halo, 0)
            return remote(perm_h.at[pl.ds(src, halo), :], px.at[pl.ds(dst, halo), :],
                          rs_sem.at[side], rr_sem.at[1 - side], target)

        def row_arrival(side, target):
            dst = 0 if side == 0 else height - halo
            return remote(perm_h.at[pl.ds(0, halo), :], px.at[pl.ds(dst, halo), :],
                          rs_sem.at[side], rr_sem.at[side], target)

        def pk_copy(side, target, rb):
            return remote(pk.at[side, rb], pr.at[1 - side, rb], ps_sem.at[side, rb], pr_sem.at[1 - side, rb], target)

        def pk_arrival(side, target, rb):
            return remote(pk.at[side, rb], pr.at[side, rb], ps_sem.at[side, rb], pr_sem.at[side, rb], target)

        def hk_copy(side, target):
            return remote(hk, hr.at[1 - side], hs_sem.at[side], hr_sem.at[1 - side], target)

        def hk_arrival(side, target):
            return remote(hk, hr.at[side], hs_sem.at[side], hr_sem.at[side], target)

        def z_copy(side, target, rb):
            strip = 0 if side == 0 else strips - 1
            return remote(s.at[rb, strip], rz.at[1 - side, rb], zs_sem.at[0, side, rb], zr_sem.at[0, 1 - side, rb], target)

        def z_arrival(side, target, rb):
            return remote(s.at[rb, 0], rz.at[side, rb], zs_sem.at[0, side, rb], zr_sem.at[0, side, rb], target)

        def x_copy(side, target):
            rb = 0 if side == 0 else last
            return remote(s.at[rb], rx.at[1 - side], xs_sem.at[0, side], xr_sem.at[0, 1 - side], target)

        def x_arrival(side, target):
            return remote(s.at[0], rx.at[side], xs_sem.at[0, side], xr_sem.at[0, side], target)

        def pair(rb, side):
            return rec.at[rb, side, :, pl.ds(0 if side == 0 else ny - 2, 2)]

        def e_copy(side, target, rb):
            return remote(pair(rb, side), got.at[1 - side, rb], zs_sem.at[1, side, rb], zr_sem.at[1, 1 - side, rb], target)

        def e_arrival(side, target, rb):
            return remote(pair(rb, side), got.at[side, rb], zs_sem.at[1, side, rb], zr_sem.at[1, side, rb], target)

        def c_copy(side, target):
            src, dst, part = (0, last, 1) if side == 0 else (last, 0, 0)
            return remote(rec.at[src, :, part], rec.at[dst, :, part], xs_sem.at[1, side], xr_sem.at[1, 1 - side], target)

        def c_arrival(side, target):
            rb, part = (0, 0) if side == 0 else (last, 1)
            return remote(rec.at[rb, :, part], rec.at[rb, :, part], xs_sem.at[1, side], xr_sem.at[1, side], target)

        def each(sides, act):
            for side, has, target in sides:
                @pl.when(has)
                def _():
                    act(side, target)

        barrier = pltpu.get_barrier_semaphore()
        each(z_sides + x_sides, lambda side, target: pl.semaphore_signal(
            barrier, inc=1, device_id=target, device_id_type=MESH))

        own = pltpu.make_async_copy(perm_h, px.at[pl.ds(halo, length), :], p_sem)
        own.start()

        @pl.loop(0, nx)
        def _(k):
            i = pick(k, [0, nx - 1, 1, nx - 2] + list(range(2, nx - 2)))
            a_copy(i, 0).start()
            a_copy(i, 1).start()

        edge = jnp.zeros((PAD, half), jnp.float32)

        @pl.loop(0, nx)
        def _(i):
            for buf in (a, b):
                for j in range(ny):
                    for h in range(2):
                        buf[i + 1, j, h, 0:PAD, :] = edge
                        buf[i + 1, j, h, PAD + full:, :] = edge

        for buf in (a, b):
            for j in range(ny):
                for h in range(2):
                    buf[0, j, h, half:, :] = jnp.zeros((2 * PAD + half, half), jnp.float32)
                    buf[nx + 1, j, h, 0:2 * PAD + half, :] = jnp.zeros((2 * PAD + half, half), jnp.float32)

        for side, has, _t in z_sides:
            @pl.when(jnp.logical_not(has))
            def _():
                @pl.loop(0, nx + 1)
                def _(rb):
                    rz[side, rb] = jnp.zeros((half, half), jnp.float32)
                    got[side, rb] = jnp.zeros((2, 2, PAD, half), jnp.float32)
                    pr[side, rb] = jnp.zeros((hw + PAD, half), jnp.float32)
                hr[side] = jnp.zeros((2, PAD, half), jnp.float32)

        for side, has, _t in x_sides:
            @pl.when(jnp.logical_not(has))
            def _():
                lo = 0 if side == 0 else height - halo
                px[lo:lo + halo, :] = jnp.zeros((halo, full), jnp.float32)
                rb, part = (0, 0) if side == 0 else (last, 1)
                rec[rb, :, part] = jnp.zeros((2, ny, PAD, half), jnp.float32)

        lane = lax.broadcasted_iota(jnp.int32, (hw, half), 1)
        low_half = lane < hw
        lane8 = lax.broadcasted_iota(jnp.int32, (PAD, half), 1)

        def shifted_rows(lo, count):
            return pltpu.roll(px[pl.ds(lo, count), :], hw, 1)

        def pack(rb):
            lo = pl.multiple_of(rb * half + PAD, PAD)
            first = shifted_rows(lo, hw)
            second = shifted_rows(lo + hw, hw)
            m0, m1 = first[:, :half], second[:, :half]
            for n, part in ((0, first), (1, second)):
                pe[1, pl.ds(lo + n * hw, hw), :] = part[:, :half]
                pe[2, pl.ds(lo + n * hw, hw), :] = part[:, half:]
            pk[1, rb, 0:hw, :] = jnp.where(low_half, m0, pltpu.roll(m1, hw, 1))
            pk[0, rb, 0:hw, :] = jnp.where(low_half, pltpu.roll(m0, hw, 1), m1)
            to_left = jnp.zeros((PAD, half), jnp.float32)
            to_right = to_left
            for k in range(half // PAD):
                part = first if k * PAD < hw else second
                q = k * PAD % hw
                e = part[q:q + PAD, half:]
                here = lane8 == k
                to_left = jnp.where(here, pltpu.roll(e, k, 1) if k else e, to_left)
                to_right = jnp.where(here, pltpu.roll(e, k + 1, 1), to_right)
            pk[0, rb, hw:hw + PAD, :] = to_left
            pk[1, rb, hw:hw + PAD, :] = to_right
            each(z_sides, lambda side, target: pk_copy(side, target, rb).start())

        ends = ((0, 0), (1, height - PAD))

        def pack_ends():
            for n, lo in ends:
                rolled = shifted_rows(lo, PAD)
                hk[n] = rolled[:, :half]
                pe[2, lo:lo + PAD, :] = rolled[:, half:]
            each(z_sides, lambda side, target: hk_copy(side, target).start())

        def unpack(rb):
            each(z_sides, lambda side, target: pk_arrival(side, target, rb).wait_recv())
            lo = pl.multiple_of(rb * half + PAD, PAD)
            from_left, from_right = pr[0, rb, 0:hw, :], pr[1, rb, 0:hw, :]
            for n in range(2):
                start = lo + n * hw
                m = pe[1, pl.ds(start, hw), :]
                fl = pltpu.roll(from_left, hw, 1) if n else from_left
                fr = from_right if n else pltpu.roll(from_right, hw, 1)
                pe[1, pl.ds(start, hw), :] = jnp.where(low_half, fl, m)
                pe[3, pl.ds(start, hw), :] = jnp.where(low_half, m, fr)
            cl, cr = pr[0, rb, hw:hw + PAD, :], pr[1, rb, hw:hw + PAD, :]
            for k in range(half // PAD):
                pe[0, pl.ds(lo + k * PAD, PAD), :] = pltpu.roll(cl, half - 1 - k, 1)
                pe[4, pl.ds(lo + k * PAD, PAD), :] = pltpu.roll(cr, half - k, 1) if k else cr

        def unpack_ends():
            each(z_sides, lambda side, target: hk_arrival(side, target).wait_recv())
            low8 = lane8 < hw
            for n, lo in ends:
                pe[1, lo:lo + PAD, :] = jnp.where(low8, hr[0, n], hk[n])
                pe[3, lo:lo + PAD, :] = jnp.where(low8, hk[n], hr[1, n])

        lane_h = lax.broadcasted_iota(jnp.int32, (CH, half), 1)
        row_h = lax.broadcasted_iota(jnp.int32, (CH, half), 0)
        first_lane, last_lane = lane_h == 0, lane_h == half - 1

        def ahead(x):
            return pltpu.roll(x, half - 1, 1)

        def behind(x):
            return pltpu.roll(x, 1, 1)

        def weigh(rb):
            base = pl.multiple_of(rb * half + PAD, PAD)
            for r in range(0, half, CH):
                mids = [pe[c, pl.ds(base + r, CH), :] for c in range(strips + 2)]
                fores = [ahead(x) if c else None for c, x in enumerate(mids)]
                afts = [behind(x) if c < strips + 1 else None for c, x in enumerate(mids)]
                for c in range(1, strips + 1):
                    mid = mids[c]
                    east = pe[c, pl.ds(base + r + 1, CH), :]
                    west = pe[c, pl.ds(base + r - 1, CH), :]
                    north = jnp.where(last_lane, fores[c + 1], fores[c])
                    south = jnp.where(first_lane, afts[c - 1], afts[c])
                    se, sw, sn, ss = mid + east, mid + west, mid + north, mid + south
                    across, along = sn * ss, se * sw
                    ne, nw = east * sw * across, west * se * across
                    nn, ns = north * ss * along, south * sn * along
                    scale = coupling / jnp.maximum((ne + nw) + (nn + ns), 1e-30)
                    for n, face in enumerate((ne, nw, nn, ns)):
                        w[n, rb, c - 1, r:r + CH, :] = face * scale

        def accumulate(store, c, value):
            store[c] = value if store[c] is None else store[c] + value

        def update(src, rb, r, part, j):
            lo = PAD + r + (half if part == 0 else 0)
            xs = [src[rb + part, j, h, lo:lo + CH, :] for h in range(2)]
            fores, afts = [ahead(x) for x in xs], [behind(x) for x in xs]
            fore = (jnp.where(last_lane, fores[1], fores[0]), jnp.where(last_lane, 0.0, fores[1]))
            aft = (jnp.where(first_lane, 0.0, afts[0]), jnp.where(first_lane, afts[0], afts[1]))
            news = []
            for h in range(2):
                c = j + h
                new = xs[h] + w[0, rb, c, r:r + CH, :] * src[rb + part, j, h, lo + 1:lo + 1 + CH, :]
                new = new + w[1, rb, c, r:r + CH, :] * src[rb + part, j, h, lo - 1:lo - 1 + CH, :]
                new = new + w[2, rb, c, r:r + CH, :] * fore[h]
                news.append(new + w[3, rb, c, r:r + CH, :] * aft[h])
            return lo, xs, news, fores[1], afts[1], fores[0], afts

        def smooth_first(rb):
            for r in range(0, half, CH):
                total = [None] * strips
                for part in range(2):
                    for j in range(ny):
                        lo, xs, news, *_ = update(a, rb, r, part, j)
                        for h in range(2):
                            value = jnp.where(xs[h] > 0, news[h], 0.0)
                            b[rb + part, j, h, lo:lo + CH, :] = value
                            accumulate(total, j + h, value)
                for c in range(strips):
                    s[rb, c, r:r + CH, :] = total[c]

        def smooth_second(rb):
            for r in range(0, half, CH):
                lost = [None] * strips
                for part in range(2):
                    for j in range(ny):
                        lo, xs, news, _, aft_end, fore_start, _a = update(b, rb, r, part, j)
                        for h in range(2):
                            mask = a[rb + part, j, h, lo:lo + CH, :] > 0
                            d[rb + part, j, h, lo:lo + CH, :] = jnp.where(mask, news[h], 0.0)
                            accumulate(lost, j + h, jnp.where(mask, 0.0, news[h]))
                        if j + 2 < strips:
                            accumulate(lost, j + 2, w[3, rb, j + 2, r:r + CH, :] * jnp.where(first_lane, aft_end, 0.0))
                        if j >= 1:
                            accumulate(lost, j - 1, w[2, rb, j - 1, r:r + CH, :] * jnp.where(last_lane, fore_start, 0.0))
                for c in range(strips):
                    lk[rb, c, r:r + CH, :] = lost[c]

        def normalise(rb):
            each(z_sides, lambda side, target: z_arrival(side, target, rb).wait_recv())
            for c in range(strips):
                for r in range(0, half, CH):
                    total = s[rb, c, r:r + CH, :]
                    if c == 0:
                        total = total + rz[0, rb, r:r + CH, :]
                    if c == strips - 1:
                        total = total + rz[1, rb, r:r + CH, :]
                    scale = 1.0 / jnp.where(total > 0, total, 1.0)
                    for j, h in ((c - 1, 1), (c, 0)):
                        if 0 <= j < ny:
                            for part in range(2):
                                lo = PAD + r + (half if part == 0 else 0)
                                b[rb + part, j, h, lo:lo + CH, :] = b[rb + part, j, h, lo:lo + CH, :] * scale

        diagonal = lax.broadcasted_iota(jnp.int32, (half, half), 0) == lax.broadcasted_iota(jnp.int32, (half, half), 1)

        def record(rb, part):
            off = PAD + (half if part == 0 else 0)
            for side in range(2):
                for j in range(ny):
                    x = b[rb + part, j, side, off:off + half, :]
                    inside = jnp.where(a[rb + part, j, side, PAD + half:PAD + half + 1, :] > 0, 1.0, 0.0)
                    beyond = jnp.where(inside > 0, 0.0, ahead(inside) if side == 0 else behind(inside))
                    edge_lane = behind(beyond) if side == 0 else ahead(beyond)
                    along = jnp.sum(x * edge_lane, axis=1, keepdims=True)
                    rim = x[:, 0:1] if side == 0 else x[:, half - 1:half]
                    q = off + half - NEAR if part == 0 else off
                    beside = 1 if part == 0 else -1
                    near = b[rb + part, j, side, q:q + NEAR, :]
                    here = a[rb + part, j, side, q:q + NEAR, :]
                    over = a[rb + part, j, side, q + beside:q + beside + NEAR, :]
                    count = jnp.sum(jnp.where(here > 0, 1.0, 0.0), axis=0, keepdims=True)
                    place = count + (half - NEAR) if part == 0 else (NEAR - 1) - count
                    flat = jnp.sum(jnp.where(over > 0, 0.0, near), axis=0, keepdims=True)
                    rows = (jnp.sum(jnp.where(diagonal, along, 0.0), axis=0, keepdims=True), beyond, flat, place,
                            jnp.sum(jnp.where(diagonal, rim, 0.0), axis=0, keepdims=True))
                    for n, value in enumerate(rows):
                        rec[rb, side, part, j, n:n + 1, :] = value
                    rec[rb, side, part, j, len(rows):, :] = jnp.zeros((PAD - len(rows), half), jnp.float32)

        def past(value, part):
            return jnp.where(value[3:4] == (half if part == 0 else -1), value[2:3], 0.0)

        def e_send(rb):
            each(z_sides, lambda side, target: e_copy(side, target, rb).start())

        def c_send(side):
            _, has, target = x_sides[side]
            rb, part, before = (0, 1, 1) if side == 0 else (last, 0, last - 1)

            @pl.when(has)
            def _():
                for edge_side in range(2):
                    for j in range(ny):
                        rec[rb, edge_side, part, j, 5:6, :] = past(rec[before, edge_side, part, j], part)
                c_copy(side, target).start()

        def spread(value, r):
            return jnp.sum(jnp.where(lane_h == row_h + r, value, 0.0), axis=1, keepdims=True)

        def lose_edge(rb, c, r, value, side, part):
            out = w[2 if side == 0 else 3, rb, c, r:r + CH, :] * (spread(value[0:1], r) * value[1:2])
            if (r + CH > half - NEAR) if part == 0 else (r < NEAR):
                line = jnp.where((row_h + r).astype(jnp.float32) == value[3:4], value[2:3], 0.0)
                out = out + w[1 - part, rb, c, r:r + CH, :] * line
            return out

        def lose_rim(rb, c, r, values, side):
            rim_lane = last_lane if side == 0 else first_lane
            return w[2 if side == 0 else 3, rb, c, r:r + CH, :] * jnp.where(rim_lane, spread(values, r), 0.0)

        def lose_rows(rb, part):
            for side in range(2):
                for j in range(ny):
                    value = rec[rb, side, part, j]
                    c = j + side
                    other = c + (1 if side == 1 else -1)
                    for r in range(0, half, CH):
                        lk[rb, c, r:r + CH, :] = lk[rb, c, r:r + CH, :] + lose_edge(rb, c, r, value, side, part)
                        if 0 <= other < strips:
                            lk[rb, other, r:r + CH, :] = lk[rb, other, r:r + CH, :] + lose_rim(rb, other, r, value[4:5], side)

        def passed(store, rb, part):
            if part == 0:
                return jnp.where(rb > 0, past(store(jnp.maximum(rb - 1, 0)), 0), store(rb)[5:6])
            return jnp.where(rb < nx, past(store(jnp.minimum(rb + 1, nx)), 1), store(rb)[5:6])

        def resolve(rb):
            @pl.when(rb == 0)
            def _():
                lose_rows(0, 0)

            @pl.when(rb == nx)
            def _():
                lose_rows(nx, 1)

            for c in range(strips):
                for r in range(0, half, CH):
                    lost = lk[rb, c, r:r + CH, :]
                    for z, k, side, own in ((0, 1, 1, 0), (1, 0, 0, strips - 1)):
                        if c == own:
                            for part in range(2):
                                lost = lost + lose_edge(rb, c, r, got[z, rb, part, k], side, part)
                            rim = got[z, rb, 0, 1 - k, 4:5, :] + got[z, rb, 1, 1 - k, 4:5, :]
                            lost = lost + lose_rim(rb, c, r, rim, side)
                        if c == own + (1 if side == 1 else -1):
                            rim = got[z, rb, 0, k, 4:5, :] + got[z, rb, 1, k, 4:5, :]
                            lost = lost + lose_rim(rb, c, r, rim, side)
                    for part, row in ((0, 0), (1, half - 1)):
                        if r <= row < r + CH:
                            over = [None]
                            for side, j, z, k in ((1, c - 1, 0, 1), (0, c, 1, 0)):
                                if 0 <= j < ny:
                                    accumulate(over, 0, passed(lambda q: rec[q, side, part, j], rb, part))
                                else:
                                    accumulate(over, 0, passed(lambda q: got[z, q, part, k], rb, part))
                            lost = lost + w[1 - part, rb, c, r:r + CH, :] * jnp.where(row_h + r == row, over[0], 0.0)
                    scale = 1.0 / ((1.0 + coupling) - lost)
                    for j, h in ((c - 1, 1), (c, 0)):
                        if 0 <= j < ny:
                            for part in range(2):
                                lo = PAD + r + (half if part == 0 else 0)
                                d[rb + part, j, h, lo:lo + CH, :] = d[rb + part, j, h, lo:lo + CH, :] * scale

        def o_each(rb, act):
            for part, inside in ((0, rb > 0), (1, rb < nx)):
                @pl.when(inside)
                def _():
                    for h in range(2):
                        act(o_copy(rb, part, h))

        peers = sum(jnp.where(has, 1, 0) for _, has, _t in z_sides + x_sides)
        pl.semaphore_wait(barrier, peers)

        each(x_sides, lambda side, target: row_copy(side, target).start())
        own.wait()

        @pl.loop(0, nx + 1)
        def _(k):
            rb = pick(k, pack_order)

            @pl.when(rb == 0)
            def _():
                each(x_sides, lambda side, target: row_arrival(side, target).wait_recv())
                pack_ends()

            pack(rb)

        @pl.loop(0, nx)
        def _(i):
            a_copy(i, 0).wait()
            a_copy(i, 1).wait()

        for n, rb in enumerate(unpack_steps[0]):
            unpack(rb)
        unpack_ends()
        width = max(len(n) for n in unpack_steps[1:])

        @pl.loop(0, nx + 1)
        def _(k):
            rb = pick(k, weigh_order)
            for q in range(width):
                new = pick(k, [-1] + [n[q] if q < len(n) else -1 for n in unpack_steps[1:]])

                @pl.when(new >= 0)
                def _():
                    unpack(new)

            weigh(rb)
            smooth_first(rb)

            for side, at in ((0, 0), (1, nx)):
                @pl.when(rb == at)
                def _():
                    _, has, target = x_sides[side]

                    @pl.when(has)
                    def _():
                        x_copy(side, target).start()

            @pl.when(jnp.logical_and(rb > 0, rb < nx))
            def _():
                each(z_sides, lambda side, target: z_copy(side, target, rb).start())

            @pl.when(rb == 3)
            def _():
                for side, at in ((0, 0), (1, nx)):
                    _, has, target = x_sides[side]

                    @pl.when(has)
                    def _():
                        x_copy(side, target).wait_send()
                        x_arrival(side, target).wait_recv()
                        for c in range(strips):
                            s[at, c] = s[at, c] + rx[side, c]
                    each(z_sides, lambda z, to: z_copy(z, to, at).start())

        @pl.loop(0, len(events))
        def _(k):
            rb = pick(k, [n for n, _ in events])

            @pl.when(rb >= 0)
            def _():
                normalise(rb)

                @pl.when(rb > 0)
                def _():
                    record(rb, 0)

                @pl.when(rb < nx)
                def _():
                    record(rb, 1)

                for side, at in ((0, 0), (1, nx)):
                    @pl.when(rb == at)
                    def _():
                        c_send(side)

                @pl.when(jnp.logical_and(rb > 0, rb < nx))
                def _():
                    e_send(rb)

            again = pick(k, [n for _, n in events])

            @pl.when(again >= 0)
            def _():
                smooth_second(again)

            @pl.when(k == nx - 1)
            def _():
                def arrive(side, target):
                    c_copy(side, target).wait_send()
                    c_arrival(side, target).wait_recv()
                each(x_sides, arrive)
                e_send(0)
                e_send(nx)

        width = max(len(n) for n in resolve_steps)

        @pl.loop(0, nx + 1)
        def _(k):
            for q in range(width):
                new = pick(k, [n[q] if q < len(n) else -1 for n in resolve_steps])

                @pl.when(new >= 0)
                def _():
                    each(z_sides, lambda side, target: e_arrival(side, target, new).wait_recv())

            rb = pick(k, resolve_order)
            resolve(rb)
            o_each(rb, lambda copy: copy.start())

        @pl.loop(0, nx + 1)
        def _(rb):
            o_each(rb, lambda copy: copy.wait())

        def drain(side, target):
            @pl.loop(0, nx + 1)
            def _(rb):
                z_copy(side, target, rb).wait_send()
                e_copy(side, target, rb).wait_send()
                pk_copy(side, target, rb).wait_send()
            hk_copy(side, target).wait_send()
        each(z_sides, drain)
        each(x_sides, lambda side, target: row_copy(side, target).wait_send())

    return kernel


def local(permeability, basis, support):
    nx, ny, full, _ = basis.shape
    half = full // 2
    size_x, size_y = lax.axis_size("gx"), lax.axis_size("gy")
    height = permeability.shape[0] + half + 2 * PAD
    f32 = jnp.float32
    strips = ny + 1
    boxes = pltpu.VMEM((nx + 2, ny, 2, full + 2 * PAD, half), f32)
    scratch = [
        boxes, boxes, boxes,
        pltpu.VMEM((4, nx + 1, strips, half, half), f32),
        pltpu.VMEM((nx + 1, strips, half, half), f32),
        pltpu.VMEM((nx + 1, strips, half, half), f32),
        pltpu.VMEM((2, nx + 1, half, half), f32),
        pltpu.VMEM((2, strips, half, half), f32),
        pltpu.VMEM((nx + 1, 2, 2, ny, PAD, half), f32),
        pltpu.VMEM((2, nx + 1, 2, 2, PAD, half), f32),
        pltpu.VMEM((height, full), f32),
        pltpu.VMEM((strips + 2, height, half), f32),
        pltpu.VMEM((2, nx + 1, half // 2 + PAD, half), f32),
        pltpu.VMEM((2, nx + 1, half // 2 + PAD, half), f32),
        pltpu.VMEM((2, PAD, half), f32),
        pltpu.VMEM((2, 2, PAD, half), f32),
        pltpu.SemaphoreType.DMA((nx, 2)),
        pltpu.SemaphoreType.DMA,
        pltpu.SemaphoreType.DMA((nx + 1, 2, 2)),
        pltpu.SemaphoreType.DMA((2, 2, nx + 1)),
        pltpu.SemaphoreType.DMA((2, 2, nx + 1)),
        pltpu.SemaphoreType.DMA((2, 2)),
        pltpu.SemaphoreType.DMA((2, 2)),
        pltpu.SemaphoreType.DMA((2, nx + 1)),
        pltpu.SemaphoreType.DMA((2, nx + 1)),
        pltpu.SemaphoreType.DMA((2,)),
        pltpu.SemaphoreType.DMA((2,)),
        pltpu.SemaphoreType.DMA((2,)),
        pltpu.SemaphoreType.DMA((2,)),
    ]
    return pl.pallas_call(
        make_kernel(nx, ny, size_x, size_y, half),
        out_shape=jax.ShapeDtypeStruct(basis.shape, f32),
        in_specs=[pl.BlockSpec(memory_space=pltpu.HBM)] * 2,
        out_specs=pl.BlockSpec(memory_space=pl.ANY),
        scratch_shapes=scratch,
        compiler_params=pltpu.CompilerParams(
            collective_id=0, has_side_effects=True, vmem_limit_bytes=48 * 1024 * 1024),
        name="smoothing",
    )(*[pltpu.with_memory_space_constraint(x, pltpu.HBM) for x in (permeability, basis)])


def solution(mesh):
    placed = (P("gx", "gy"), P("gx", "gy", None, None), P("gx", "gy", None, None))
    return jax.shard_map(
        local, mesh=mesh, in_specs=placed, out_specs=P("gx", "gy", None, None), check_vma=False
    )
```

profile of v0, /device:TPU:12, one launch (start us, length us, event | category | flops | bytes accessed | tf_op | source)
XLA Modules:
  0.0 35.8 jit_solution(4200211733319741548)
XLA Ops:
  0.0 33.8 %smoothing.1 = f32[8,2,256,256]{3,2,1,0:T(8,128)S(1)} custom-call(f32[1024,256]{1,0:T(8,128)} %refs_0_.1, f32[8,2,256,256]{3,2,1,0:T(8,128)} %refs_1_.1), custom_call_target="tpu_custom_call" | custom-call | tf_op jit(solution)/shard_map/smoothing/pallas_call | solution.py:640
  33.8 2.0 %copy.4 = f32[8,2,256,256]{3,2,1,0:T(8,128)} copy(f32[8,2,256,256]{3,2,1,0:T(8,128)S(1)} %smoothing.1) | data formatting | bytes 8388608
where the time goes:
time: 36.2 us; the launch traced here: 35.8 us
  Pallas kernels  33.8 us (93%)
  local copies, waits for them, and re-layouts  2.02 us (6%)
    pallas_call x1, Pallas kernels, local(): pl.pallas_call(make_kernel(nx, ny, size_x, size_y, half), out_shape=jax.S...  33.8 us
    unnamed x1, local copies, waits for them, and re-layouts  2.02 us

commit v1 on v0

v1 whole, which is shorter than its diff:
```python
import jax
import jax.numpy as jnp
from jax import lax
from jax.experimental import pallas as pl
from jax.experimental.pallas import tpu as pltpu
from jax.sharding import PartitionSpec as P

MESH = pl.DeviceIdType.MESH
relaxation = 2.0 / 3.0
coupling = relaxation / (1.0 - relaxation)
PAD = 8
CH = 32
NEAR = 40


def pick(k, table):
    value = jnp.int32(table[-1])
    for n in range(len(table) - 2, -1, -1):
        value = jnp.where(k == n, table[n], value)
    return value


def first_needs(order, count):
    seen, out = set(), []
    for rb in order:
        new = [q for q in (rb - 1, rb, rb + 1) if 0 <= q < count and q not in seen]
        seen.update(new)
        out.append(new)
    return out


def make_kernel(nx, ny, size_x, size_y, half):
    full = 2 * half
    last = nx
    strips = ny + 1
    hw = half // 2

    pack_order = [1, 2, 0, nx - 1, nx - 2, nx] + list(range(3, nx - 2))
    weigh_order = [1, nx - 1] + list(range(2, nx - 1)) + [0, nx]
    assert sorted(weigh_order) == sorted(pack_order) == list(range(nx + 1))
    unpack_steps = first_needs(weigh_order, nx + 1)
    events, done, known = [], set(), set()
    for n, rb in enumerate(weigh_order):
        known.add(rb)
        allowed = list(range(1, nx)) + ([0, nx] if n >= nx - 1 else [])
        ready = [q for q in allowed if q not in done and {m for m in (q - 1, q, q + 1) if 0 <= m <= nx} <= known][:3]
        done.update(ready)
        events += [(rb, ready[0] if ready else -1)] + [(-1, q) for q in ready[1:]]
    assert sorted(q for _, q in events if q >= 0) == list(range(nx + 1))
    first_end = min(k for k, (_, q) in enumerate(events) if q in (0, nx))
    early = [n for n, _ in events].index(3)

    def kernel(*refs):
        (perm_h, basis_h, out_h,
         a, b, d, w, s, iv, rz, xrow, zrow, far, px, pm, pe, pk, pr, hk, hr,
         a_sem, p_sem, o_sem, zs_sem, zr_sem, gs_sem, gr_sem, cs_sem, cr_sem, fs_sem, fr_sem,
         ps_sem, pr_sem, hs_sem, hr_sem, rs_sem, rr_sem) = refs
        gx, gy = lax.axis_index("gx"), lax.axis_index("gy")
        has_up, has_down = gx > 0, gx < size_x - 1
        has_left, has_right = gy > 0, gy < size_y - 1
        up, down = (gx - 1, gy), (gx + 1, gy)
        left, right = (gx, gy - 1), (gx, gy + 1)
        z_sides = ((0, has_left, left), (1, has_right, right))
        x_sides = ((0, has_up, up), (1, has_down, down))
        halo = hw + PAD
        height = px.shape[0]
        length = height - 2 * halo

        def remote(src, dst, send, recv, target):
            return pltpu.make_async_remote_copy(
                src_ref=src, dst_ref=dst, send_sem=send, recv_sem=recv, device_id=target, device_id_type=MESH)

        def a_copy(i, h):
            return pltpu.make_async_copy(
                basis_h.at[i, :, :, pl.ds(h * half, half)], a.at[i + 1, :, h, pl.ds(PAD, full), :], a_sem.at[i, h])

        def o_copy(rb, part, h):
            lo = half if part == 0 else 0
            return pltpu.make_async_copy(
                d.at[rb + part, :, h, pl.ds(PAD + lo, half), :],
                out_h.at[rb - 1 + part, :, pl.ds(lo, half), pl.ds(h * half, half)], o_sem.at[rb, part, h])

        def row_copy(side, target):
            src, dst = (0, height - halo) if side == 0 else (length - halo, 0)
            return remote(perm_h.at[pl.ds(src, halo), :], px.at[pl.ds(dst, halo), :],
                          rs_sem.at[side], rr_sem.at[1 - side], target)

        def row_arrival(side, target):
            dst = 0 if side == 0 else height - halo
            return remote(perm_h.at[pl.ds(0, halo), :], px.at[pl.ds(dst, halo), :],
                          rs_sem.at[side], rr_sem.at[side], target)

        def pk_copy(side, target, rb):
            return remote(pk.at[side, rb], pr.at[1 - side, rb], ps_sem.at[side, rb], pr_sem.at[1 - side, rb], target)

        def pk_arrival(side, target, rb):
            return remote(pk.at[side, rb], pr.at[side, rb], ps_sem.at[side, rb], pr_sem.at[side, rb], target)

        def hk_copy(side, target):
            return remote(hk, hr.at[1 - side], hs_sem.at[side], hr_sem.at[1 - side], target)

        def hk_arrival(side, target):
            return remote(hk, hr.at[side], hs_sem.at[side], hr_sem.at[side], target)

        def z_copy(side, target, rb):
            strip = 0 if side == 0 else strips - 1
            return remote(s.at[rb, strip], rz.at[1 - side, rb], zs_sem.at[side, rb], zr_sem.at[1 - side, rb], target)

        def z_arrival(side, target, rb):
            return remote(s.at[rb, 0], rz.at[side, rb], zs_sem.at[side, rb], zr_sem.at[side, rb], target)

        def g_copy(side, target, h):
            i, lo, to = (0, 0, nx + 1) if side == 0 else (nx - 1, half - PAD, 0)
            return remote(basis_h.at[i, :, pl.ds(lo, half + PAD), pl.ds(h * half, half)],
                          a.at[to, :, h, pl.ds(PAD + lo, half + PAD), :],
                          gs_sem.at[side, h], gr_sem.at[1 - side, h], target)

        def g_arrival(side, target, h):
            lo, to = (half - PAD, 0) if side == 0 else (0, nx + 1)
            return remote(basis_h.at[0, :, pl.ds(0, half + PAD), pl.ds(h * half, half)],
                          a.at[to, :, h, pl.ds(PAD + lo, half + PAD), :],
                          gs_sem.at[side, h], gr_sem.at[side, h], target)

        def c_copy(side, target):
            i, lo = (2, PAD) if side == 0 else (nx - 1, full)
            return remote(b.at[i, :, :, pl.ds(lo, PAD), :], xrow.at[1 - side], cs_sem.at[side], cr_sem.at[1 - side], target)

        def c_arrival(side, target):
            return remote(b.at[2, :, :, pl.ds(PAD, PAD), :], xrow.at[side], cs_sem.at[side], cr_sem.at[side], target)

        def f_copy(side, target, end):
            j, h = (0, 0) if side == 0 else (ny - 1, 1)
            return remote(xrow.at[end, j, h], zrow.at[1 - side, end], fs_sem.at[side, end], fr_sem.at[1 - side, end], target)

        def f_arrival(side, target, end):
            return remote(xrow.at[end, 0, 0], zrow.at[side, end], fs_sem.at[side, end], fr_sem.at[side, end], target)

        def each(sides, act):
            for side, has, target in sides:
                @pl.when(has)
                def _():
                    act(side, target)

        barrier = pltpu.get_barrier_semaphore()
        each(z_sides + x_sides, lambda side, target: pl.semaphore_signal(
            barrier, inc=1, device_id=target, device_id_type=MESH))

        own = pltpu.make_async_copy(perm_h, px.at[pl.ds(halo, length), :], p_sem)
        own.start()

        @pl.loop(0, nx)
        def _(k):
            i = pick(k, [0, nx - 1, 1, nx - 2] + list(range(2, nx - 2)))
            a_copy(i, 0).start()
            a_copy(i, 1).start()

        edge = jnp.zeros((PAD, half), jnp.float32)

        @pl.loop(0, nx)
        def _(i):
            for buf in (a, b):
                for j in range(ny):
                    for h in range(2):
                        buf[i + 1, j, h, 0:PAD, :] = edge
                        buf[i + 1, j, h, PAD + full:, :] = edge

        for buf in (a, b):
            for j in range(ny):
                for h in range(2):
                    buf[0, j, h, PAD + full:, :] = edge
                    buf[nx + 1, j, h, 0:PAD, :] = edge

        far[...] = jnp.zeros(far.shape, jnp.float32)
        for j in range(ny):
            for h in range(2):
                b[0, j, h, half:half + PAD, :] = edge
                b[nx + 1, j, h, PAD + half:2 * PAD + half, :] = edge

        for side, has, _t in z_sides:
            @pl.when(jnp.logical_not(has))
            def _():
                @pl.loop(0, nx + 1)
                def _(rb):
                    rz[side, rb] = jnp.zeros((half + PAD, half), jnp.float32)
                    pr[side, rb] = jnp.zeros((hw + PAD, half), jnp.float32)
                hr[side] = jnp.zeros((2, PAD, half), jnp.float32)
                zrow[side] = jnp.zeros((2, PAD, half), jnp.float32)

        for side, has, _t in x_sides:
            @pl.when(jnp.logical_not(has))
            def _():
                lo = 0 if side == 0 else height - halo
                px[lo:lo + halo, :] = jnp.zeros((halo, full), jnp.float32)
                lo, to = (half, 0) if side == 0 else (PAD, nx + 1)
                for j in range(ny):
                    for h in range(2):
                        a[to, j, h, lo:lo + half + PAD, :] = jnp.zeros((half + PAD, half), jnp.float32)
                xrow[side] = jnp.zeros((ny, 2, PAD, half), jnp.float32)

                for z, has_z, _z in z_sides:
                    @pl.when(has_z)
                    def _():
                        zrow[z, side] = edge

        lane = lax.broadcasted_iota(jnp.int32, (hw, half), 1)
        low_half = lane < hw
        lane8 = lax.broadcasted_iota(jnp.int32, (PAD, half), 1)

        def shifted_rows(lo, count):
            return pltpu.roll(px[pl.ds(lo, count), :], hw, 1)

        def pack(rb):
            lo = pl.multiple_of(rb * half + PAD, PAD)
            first = shifted_rows(lo, hw)
            second = shifted_rows(lo + hw, hw)
            m0, m1 = first[:, :half], second[:, :half]
            for n, part in ((0, first), (1, second)):
                pm[pl.ds(lo + n * hw, hw), :] = part[:, :half]
                pe[2, pl.ds(lo + n * hw, hw), :] = part[:, half:]
            pk[1, rb, 0:hw, :] = jnp.where(low_half, m0, pltpu.roll(m1, hw, 1))
            pk[0, rb, 0:hw, :] = jnp.where(low_half, pltpu.roll(m0, hw, 1), m1)
            to_left = jnp.zeros((PAD, half), jnp.float32)
            to_right = to_left
            for k in range(half // PAD):
                part = first if k * PAD < hw else second
                q = k * PAD % hw
                e = part[q:q + PAD, half:]
                here = lane8 == k
                to_left = jnp.where(here, pltpu.roll(e, k, 1) if k else e, to_left)
                to_right = jnp.where(here, pltpu.roll(e, k + 1, 1), to_right)
            pk[0, rb, hw:hw + PAD, :] = to_left
            pk[1, rb, hw:hw + PAD, :] = to_right
            each(z_sides, lambda side, target: pk_copy(side, target, rb).start())

        ends = ((0, 0), (1, height - PAD))

        def pack_ends():
            for n, lo in ends:
                rolled = shifted_rows(lo, PAD)
                hk[n] = rolled[:, :half]
                pm[lo:lo + PAD, :] = rolled[:, :half]
                pe[2, lo:lo + PAD, :] = rolled[:, half:]
            each(z_sides, lambda side, target: hk_copy(side, target).start())

        def unpack(rb):
            each(z_sides, lambda side, target: pk_arrival(side, target, rb).wait_recv())
            lo = pl.multiple_of(rb * half + PAD, PAD)
            from_left, from_right = pr[0, rb, 0:hw, :], pr[1, rb, 0:hw, :]
            for n in range(2):
                start = lo + n * hw
                m = pm[pl.ds(start, hw), :]
                fl = pltpu.roll(from_left, hw, 1) if n else from_left
                fr = from_right if n else pltpu.roll(from_right, hw, 1)
                pe[1, pl.ds(start, hw), :] = jnp.where(low_half, fl, m)
                pe[3, pl.ds(start, hw), :] = jnp.where(low_half, m, fr)
            cl, cr = pr[0, rb, hw:hw + PAD, :], pr[1, rb, hw:hw + PAD, :]
            for k in range(half // PAD):
                pe[0, pl.ds(lo + k * PAD, PAD), :] = pltpu.roll(cl, half - 1 - k, 1)
                pe[4, pl.ds(lo + k * PAD, PAD), :] = pltpu.roll(cr, half - k, 1) if k else cr

        def unpack_ends():
            each(z_sides, lambda side, target: hk_arrival(side, target).wait_recv())
            low8 = lane8 < hw
            for n, lo in ends:
                pe[1, lo:lo + PAD, :] = jnp.where(low8, hr[0, n], hk[n])
                pe[3, lo:lo + PAD, :] = jnp.where(low8, hk[n], hr[1, n])

        lane_h = lax.broadcasted_iota(jnp.int32, (CH, half), 1)
        row_h = lax.broadcasted_iota(jnp.int32, (CH, half), 0)
        first_lane, last_lane = lane_h == 0, lane_h == half - 1

        def ahead(x):
            return pltpu.roll(x, half - 1, 1)

        def behind(x):
            return pltpu.roll(x, 1, 1)

        def weigh(rb, chosen):
            base = pl.multiple_of(rb * half + PAD, PAD)
            for r in range(0, half, CH):
                for c in chosen:
                    inner = 0 < c < strips - 1
                    mid = pe[c + 1, pl.ds(base + r, CH), :]
                    after = pm[pl.ds(base + r, CH), :] if inner else pe[c + 2, pl.ds(base + r, CH), :]
                    before = after if inner else pe[c, pl.ds(base + r, CH), :]
                    east = pe[c + 1, pl.ds(base + r + 1, CH), :]
                    west = pe[c + 1, pl.ds(base + r - 1, CH), :]
                    north = ahead(jnp.where(first_lane, after, mid))
                    south = behind(jnp.where(last_lane, before, mid))
                    se, sw, sn, ss = mid + east, mid + west, mid + north, mid + south
                    across, along = sn * ss, se * sw
                    ne, nw = east * sw * across, west * se * across
                    nn, ns = north * ss * along, south * sn * along
                    scale = coupling / jnp.maximum((ne + nw) + (nn + ns), 1e-30)
                    for n, face in enumerate((ne, nw, nn, ns)):
                        w[n, rb, c, r:r + CH, :] = face * scale

        def accumulate(store, c, value):
            store[c] = value if store[c] is None else store[c] + value

        def update(src, rb, r, part, j):
            lo = PAD + r + (half if part == 0 else 0)
            xs = [src[rb + part, j, h, lo:lo + CH, :] for h in range(2)]
            fores, afts = [ahead(x) for x in xs], [behind(x) for x in xs]
            fore = (jnp.where(last_lane, fores[1], fores[0]), jnp.where(last_lane, 0.0, fores[1]))
            aft = (jnp.where(first_lane, 0.0, afts[0]), jnp.where(first_lane, afts[0], afts[1]))
            news = []
            for h in range(2):
                c = j + h
                new = xs[h] + w[0, rb, c, r:r + CH, :] * src[rb + part, j, h, lo + 1:lo + 1 + CH, :]
                new = new + w[1, rb, c, r:r + CH, :] * src[rb + part, j, h, lo - 1:lo - 1 + CH, :]
                new = new + w[2, rb, c, r:r + CH, :] * fore[h]
                news.append(new + w[3, rb, c, r:r + CH, :] * aft[h])
            return lo, xs, news, fores[1], afts[1], fores[0], afts

        def smooth_first(rb, chosen):
            for r in range(0, half, CH):
                for c in chosen:
                    total = [None]
                    faces = [w[n, rb, c, r:r + CH, :] for n in range(4)]
                    for j, h in ((c - 1, 1), (c, 0)):
                        if not 0 <= j < ny:
                            continue
                        for part in range(2):
                            lo = PAD + r + (half if part == 0 else 0)
                            x = a[rb + part, j, h, lo:lo + CH, :]
                            beside = a[rb + part, j, 1 - h, lo:lo + CH, :]
                            fore = ahead(jnp.where(first_lane, beside if h == 0 else 0.0, x))
                            aft = behind(jnp.where(last_lane, beside if h == 1 else 0.0, x))
                            new = x + faces[0] * a[rb + part, j, h, lo + 1:lo + 1 + CH, :]
                            new = new + faces[1] * a[rb + part, j, h, lo - 1:lo - 1 + CH, :]
                            new = new + faces[2] * fore + faces[3] * aft
                            value = jnp.where(x > 0, new, 0.0)
                            b[rb + part, j, h, lo:lo + CH, :] = value
                            accumulate(total, 0, value)
                    s[rb, c, r:r + CH, :] = total[0]

        def normalise(rb):
            each(z_sides, lambda side, target: z_arrival(side, target, rb).wait_recv())
            for c in range(strips):
                for r in range(0, half, CH):
                    total = s[rb, c, r:r + CH, :]
                    if c == 0:
                        total = total + rz[0, rb, r:r + CH, :]
                    if c == strips - 1:
                        total = total + rz[1, rb, r:r + CH, :]
                    scale = 1.0 / jnp.where(total > 0, total, 1.0)
                    for z, strip in ((0, 0), (1, strips - 1)):
                        if c == strip:
                            iv[z, pl.ds(pl.multiple_of(rb * half + PAD, PAD) + r, CH), :] = scale
                    for j, h in ((c - 1, 1), (c, 0)):
                        if 0 <= j < ny:
                            for part in range(2):
                                lo = PAD + r + (half if part == 0 else 0)
                                b[rb + part, j, h, lo:lo + CH, :] = b[rb + part, j, h, lo:lo + CH, :] * scale

        row_near = lax.broadcasted_iota(jnp.int32, (NEAR, half), 0)
        lane_1 = lax.broadcasted_iota(jnp.int32, (1, half), 1)
        lane_f = lane_1.astype(jnp.float32)

        def record(rb):
            for side in range(2):
                j, strip = (0, 0) if side == 0 else (ny - 1, strips - 1)
                rim_lane = 0 if side == 0 else half - 1
                rim_row = 0 if side == 0 else NEAR - 1

                def turn(value):
                    turned = jnp.transpose(value)
                    return turned[0:NEAR] if side == 0 else turned[half - NEAR:]

                rim, places, lanes = None, [], []
                for part in range(2):
                    off = PAD + (half if part == 0 else 0)
                    inside = jnp.where(a[rb + part, j, side, PAD + half - part * PAD:PAD + half - part * PAD + 1, :] > 0, 1.0, 0.0)
                    inside = jnp.sum(inside, axis=1, keepdims=True)
                    place = (half - 1.0) - inside if side == 0 else inside
                    taken = jnp.logical_or(lane_f == (place + 1.0 if side == 0 else place - 1.0), lane_1 == rim_lane)
                    turned = turn(jnp.where(taken, b[rb + part, j, side, off:off + half, :], 0.0))
                    s[rb, strip, half + part:half + part + 1, :] = jnp.sum(
                        jnp.where(row_near == rim_row, 0.0, turned), axis=0, keepdims=True)
                    value = turned[rim_row:rim_row + 1]
                    rim = value if rim is None else rim + value
                    q = off + half - NEAR if part == 0 else off
                    beside = 1 if part == 0 else -1
                    near = b[rb + part, j, side, q:q + NEAR, :]
                    here = a[rb + part, j, side, q:q + NEAR, :]
                    over = a[rb + part, j, side, q + beside:q + beside + NEAR, :]
                    count = jnp.sum(jnp.where(here > 0, 1.0, 0.0), axis=0, keepdims=True)
                    inner = count[:, half - 1:] if side == 0 else count[:, 0:1]
                    places.append(inner + (half - NEAR) if part == 0 else (NEAR - 1) - inner)
                    lanes.append(place)
                    s[rb, strip, half + 2 + part:half + 3 + part, :] = jnp.sum(jnp.where(over > 0, 0.0, near), axis=0, keepdims=True)
                other, beside = (1, 1) if side == 0 else (ny - 2, strips - 2)
                both = b[rb, other, side, PAD + half:PAD + full, :] + b[rb + 1, other, side, PAD:PAD + half, :]
                total = s[rb, beside, 0:half, :]
                both = jnp.where(lane_1 == rim_lane, both / jnp.where(total > 0, total, 1.0), 0.0)
                s[rb, strip, half + 4:half + 5, :] = turn(both)[rim_row:rim_row + 1]
                s[rb, strip, half + 5:half + 6, :] = rim
                where = jnp.zeros((1, half), jnp.float32)
                for n, value in enumerate(places + lanes):
                    where = jnp.where(lane_1 == n, value, where)
                s[rb, strip, half + 6:half + 7, :] = where
                s[rb, strip, half + 7:, :] = jnp.zeros((1, half), jnp.float32)

        def spread(value, r):
            return jnp.sum(jnp.where(lane_h == row_h + r, value, 0.0), axis=1, keepdims=True)

        row_f = row_h.astype(jnp.float32)
        lane_hf = lane_h.astype(jnp.float32)

        def finish(rb):
            inner_up, inner_down = rb > 0, rb < nx
            base = pl.multiple_of(rb * half + PAD, PAD)

            def where_of(z, q):
                line = rz[z, q, half + 6:half + 7, :]
                return [line[:, n:n + 1] for n in range(4)]

            spots = [where_of(z, rb) for z in range(2)]
            for r in range(0, half, CH):
                lost = [None] * strips
                results = [[] for _ in range(strips)]
                for part in range(2):
                    for j in range(ny):
                        lo, xs, news, _, aft_end, fore_start, _a = update(b, rb, r, part, j)
                        for h in range(2):
                            mask = a[rb + part, j, h, lo:lo + CH, :] > 0
                            results[j + h].append((part, j, h, lo, jnp.where(mask, news[h], 0.0)))
                            accumulate(lost, j + h, jnp.where(mask, 0.0, news[h]))
                        if j + 2 < strips:
                            accumulate(lost, j + 2, w[3, rb, j + 2, r:r + CH, :] * jnp.where(first_lane, aft_end, 0.0))
                        if j >= 1:
                            accumulate(lost, j - 1, w[2, rb, j - 1, r:r + CH, :] * jnp.where(last_lane, fore_start, 0.0))
                for part, row, inner in ((0, 0, inner_up), (1, half - 1, inner_down)):
                    if r <= row < r + CH:
                        for c in range(strips):
                            over = [None]
                            for j, h, z in ((c - 1, 1, 0), (c, 0, 1)):
                                if part == 0:
                                    i, at, q = jnp.maximum(rb - 1, 0), PAD + full - 1, jnp.maximum(rb - 1, 0)
                                else:
                                    i, at, q = jnp.minimum(rb + 2, nx + 1), PAD, jnp.minimum(rb + 1, nx)
                                if 0 <= j < ny:
                                    accumulate(over, 0, b[i, j, h, at:at + 1, :])
                                else:
                                    spot = rz[z, q, half + 6:half + 7, part:part + 1]
                                    there = iv[z, pl.ds(base + (-1 if part == 0 else half), 1), :]
                                    value = rz[z, q, half + 2 + part:half + 3 + part, :] * there
                                    accumulate(over, 0, jnp.where(spot == (half if part == 0 else -1), value, 0.0))
                            keep = jnp.logical_and(row_h + r == row, inner)
                            accumulate(lost, c, w[1 - part, rb, c, r:r + CH, :] * jnp.where(keep, over[0], 0.0))
                for z, side, c in ((0, 1, 0), (1, 0, strips - 1)):
                    at_rim = last_lane if side == 0 else first_lane
                    face = 2 if side == 0 else 3
                    scale = iv[z, pl.ds(base + r, CH), :]
                    shifted = ahead(scale) if side == 0 else behind(scale)
                    v = [spread(rz[z, rb, half + n:half + n + 1, :], r) for n in (0, 1, 4, 5)]
                    field = jnp.where(lane_hf == spots[z][2], v[0], 0.0) + jnp.where(lane_hf == spots[z][3], v[1], 0.0)
                    field = field * shifted + jnp.where(at_rim, v[2], 0.0)
                    accumulate(lost, c, w[face, rb, c, r:r + CH, :] * field)
                    other = c + (1 if side == 1 else -1)
                    accumulate(lost, other, w[face, rb, other, r:r + CH, :] * jnp.where(at_rim, v[3] * shifted, 0.0))
                    for part in range(2):
                        if (r + CH > half - NEAR) if part == 0 else (r < NEAR):
                            line = jnp.where(row_f + r == spots[z][part], rz[z, rb, half + 2 + part:half + 3 + part, :], 0.0)
                            there = iv[z, pl.ds(base + r + (-1 if part == 0 else 1), CH), :]
                            accumulate(lost, c, w[1 - part, rb, c, r:r + CH, :] * line * there)
                for c in range(strips):
                    extra = ends_lost(rb, c, r)
                    total = (1.0 + coupling) - (lost[c] if extra is None else lost[c] + extra)
                    scale = 1.0 / total
                    for part, j, h, lo, value in results[c]:
                        d[rb + part, j, h, lo:lo + CH, :] = value * scale

        def ends_lost(rb, c, r):
            for end, row in ((0, 0), (1, half - 1)):
                if r <= row < r + CH:
                    keep = jnp.logical_and(row_h + r == row, rb == (0 if end == 0 else nx))
                    return w[1 - end, rb, c, r:r + CH, :] * jnp.where(keep, far[end, c, 0:1, :], 0.0)
            return None

        def gather_far():
            for end in range(2):
                at = PAD - 1 if end == 0 else 0
                for c in range(strips):
                    over = [None]
                    for j, h, z in ((c - 1, 1, 0), (c, 0, 1)):
                        accumulate(over, 0, xrow[end, j, h, at:at + 1, :] if 0 <= j < ny else zrow[z, end, at:at + 1, :])
                    far[end, c, 0:1, :] = over[0]

        def o_each(rb, act):
            for part, inside in ((0, rb > 0), (1, rb < nx)):
                @pl.when(inside)
                def _():
                    for h in range(2):
                        act(o_copy(rb, part, h))

        peers = sum(jnp.where(has, 1, 0) for _, has, _t in z_sides + x_sides)
        pl.semaphore_wait(barrier, peers)

        each(x_sides, lambda side, target: row_copy(side, target).start())

        def send_boxes(side, target):
            for h in range(2):
                g_copy(side, target, h).start()
        each(x_sides, send_boxes)
        own.wait()

        @pl.loop(0, nx + 1)
        def _(k):
            rb = pick(k, pack_order)

            @pl.when(rb == 0)
            def _():
                each(x_sides, lambda side, target: row_arrival(side, target).wait_recv())
                pack_ends()

            pack(rb)

        @pl.loop(0, nx)
        def _(i):
            a_copy(i, 0).wait()
            a_copy(i, 1).wait()

        inner_strips, outer_strips = list(range(1, strips - 1)), [0, strips - 1]

        @pl.loop(1, nx)
        def _(rb):
            weigh(rb, inner_strips)
            smooth_first(rb, inner_strips)

        for n, rb in enumerate(unpack_steps[0]):
            unpack(rb)
        unpack_ends()
        width = max(len(n) for n in unpack_steps[1:])

        @pl.loop(0, nx + 1)
        def _(k):
            rb = pick(k, weigh_order)
            for q in range(width):
                new = pick(k, [-1] + [n[q] if q < len(n) else -1 for n in unpack_steps[1:]])

                @pl.when(new >= 0)
                def _():
                    unpack(new)

            weigh(rb, outer_strips)

            @pl.when(jnp.logical_or(rb == 0, rb == nx))
            def _():
                for side, at in ((0, 0), (1, nx)):
                    @pl.when(rb == at)
                    def _():
                        _, has, target = x_sides[side]

                        @pl.when(has)
                        def _():
                            for h in range(2):
                                g_arrival(side, target, h).wait_recv()
                weigh(rb, inner_strips)
                smooth_first(rb, inner_strips)

            smooth_first(rb, outer_strips)
            record(rb)
            each(z_sides, lambda side, target: z_copy(side, target, rb).start())

        @pl.loop(0, len(events))
        def _(k):
            rb = pick(k, [n for n, _ in events])

            @pl.when(rb >= 0)
            def _():
                normalise(rb)
                for side, at in ((0, 1), (1, nx - 1)):
                    @pl.when(rb == at)
                    def _():
                        _, has, target = x_sides[side]

                        @pl.when(has)
                        def _():
                            c_copy(side, target).start()

            @pl.when(k == early)
            def _():
                def forward(end, target):
                    c_copy(end, target).wait_send()
                    c_arrival(end, target).wait_recv()
                    each(z_sides, lambda side, to: f_copy(side, to, end).start())
                each(x_sides, forward)

            now = pick(k, [n for _, n in events])

            @pl.when(k == first_end)
            def _():
                each(x_sides, lambda end, target: each(z_sides, lambda side, to: f_arrival(side, to, end).wait_recv()))
                gather_far()

            @pl.when(now >= 0)
            def _():
                finish(now)
                o_each(now, lambda copy: copy.start())

        @pl.loop(0, nx + 1)
        def _(rb):
            o_each(rb, lambda copy: copy.wait())

        def drain(side, target):
            @pl.loop(0, nx + 1)
            def _(rb):
                z_copy(side, target, rb).wait_send()
                pk_copy(side, target, rb).wait_send()
            hk_copy(side, target).wait_send()
        each(z_sides, drain)

        def drain_rows(end, target):
            row_copy(end, target).wait_send()
            for h in range(2):
                g_copy(end, target, h).wait_send()
            each(z_sides, lambda side, to: f_copy(side, to, end).wait_send())
        each(x_sides, drain_rows)

    return kernel


def local(permeability, basis, support):
    nx, ny, full, _ = basis.shape
    half = full // 2
    size_x, size_y = lax.axis_size("gx"), lax.axis_size("gy")
    height = permeability.shape[0] + half + 2 * PAD
    f32 = jnp.float32
    strips = ny + 1
    boxes = pltpu.VMEM((nx + 2, ny, 2, full + 2 * PAD, half), f32)
    scratch = [
        boxes, boxes, boxes,
        pltpu.VMEM((4, nx + 1, strips, half, half), f32),
        pltpu.VMEM((nx + 1, strips, half + PAD, half), f32),
        pltpu.VMEM((2, (nx + 1) * half + 2 * PAD, half), f32),
        pltpu.VMEM((2, nx + 1, half + PAD, half), f32),
        pltpu.VMEM((2, ny, 2, PAD, half), f32),
        pltpu.VMEM((2, 2, PAD, half), f32),
        pltpu.VMEM((2, strips, PAD, half), f32),
        pltpu.VMEM((height, full), f32),
        pltpu.VMEM((height, half), f32),
        pltpu.VMEM((strips + 2, height, half), f32),
        pltpu.VMEM((2, nx + 1, half // 2 + PAD, half), f32),
        pltpu.VMEM((2, nx + 1, half // 2 + PAD, half), f32),
        pltpu.VMEM((2, PAD, half), f32),
        pltpu.VMEM((2, 2, PAD, half), f32),
        pltpu.SemaphoreType.DMA((nx, 2)),
        pltpu.SemaphoreType.DMA,
        pltpu.SemaphoreType.DMA((nx + 1, 2, 2)),
        pltpu.SemaphoreType.DMA((2, nx + 1)),
        pltpu.SemaphoreType.DMA((2, nx + 1)),
        pltpu.SemaphoreType.DMA((2, 2)),
        pltpu.SemaphoreType.DMA((2, 2)),
        pltpu.SemaphoreType.DMA((2,)),
        pltpu.SemaphoreType.DMA((2,)),
        pltpu.SemaphoreType.DMA((2, 2)),
        pltpu.SemaphoreType.DMA((2, 2)),
        pltpu.SemaphoreType.DMA((2, nx + 1)),
        pltpu.SemaphoreType.DMA((2, nx + 1)),
        pltpu.SemaphoreType.DMA((2,)),
        pltpu.SemaphoreType.DMA((2,)),
        pltpu.SemaphoreType.DMA((2,)),
        pltpu.SemaphoreType.DMA((2,)),
    ]
    return pl.pallas_call(
        make_kernel(nx, ny, size_x, size_y, half),
        out_shape=jax.ShapeDtypeStruct(basis.shape, f32),
        in_specs=[pl.BlockSpec(memory_space=pltpu.HBM)] * 2,
        out_specs=pl.BlockSpec(memory_space=pl.ANY),
        scratch_shapes=scratch,
        compiler_params=pltpu.CompilerParams(
            collective_id=0, has_side_effects=True, vmem_limit_bytes=48 * 1024 * 1024),
        name="smoothing",
    )(*[pltpu.with_memory_space_constraint(x, pltpu.HBM) for x in (permeability, basis)])


def solution(mesh):
    placed = (P("gx", "gy"), P("gx", "gy", None, None), P("gx", "gy", None, None))
    return jax.shard_map(
        local, mesh=mesh, in_specs=placed, out_specs=P("gx", "gy", None, None), check_vma=False
    )
```

time: 36.2 us -> 34.2 us (0.945)
  Pallas kernels: 33.8 us -> 31.8 us
    pallas_call x1, Pallas kernels: 33.8 us -> 31.8 us  [local(): pl.pallas_call(make_kernel(nx, ny, size_x, size_y, half), out_shape=jax.S...]
where the time goes in v1:
time: 34.2 us; the launch traced here: 33.8 us
  Pallas kernels  31.8 us (93%)
  local copies, waits for them, and re-layouts  2.02 us (6%)
    pallas_call x1, Pallas kernels, local(): pl.pallas_call(make_kernel(nx, ny, size_x, size_y, half), out_shape=jax.S...  31.8 us
    unnamed x1, local copies, waits for them, and re-layouts  2.02 us

profile of v1, /device:TPU:12, one launch (start us, length us, event | category | flops | bytes accessed | tf_op | source)
XLA Modules:
  0.0 33.8 jit_solution(4121910003944369756)
XLA Ops:
  0.0 31.8 %smoothing.1 = f32[8,2,256,256]{3,2,1,0:T(8,128)S(1)} custom-call(f32[1024,256]{1,0:T(8,128)} %refs_0_.1, f32[8,2,256,256]{3,2,1,0:T(8,128)} %refs_1_.1), custom_call_target="tpu_custom_call" | custom-call | tf_op jit(solution)/shard_map/smoothing/pallas_call | solution.py:667
  31.8 2.0 %copy.4 = f32[8,2,256,256]{3,2,1,0:T(8,128)} copy(f32[8,2,256,256]{3,2,1,0:T(8,128)S(1)} %smoothing.1) | data formatting | bytes 8388608

commit v2 on v1

--- a/solution.py
+++ b/solution.py
@@ -9,7 +9,7 @@
 relaxation = 2.0 / 3.0
 coupling = relaxation / (1.0 - relaxation)
 PAD = 8
-CH = 32
+CH = 64
 NEAR = 40
 
 

time: 34.2 us -> 34.1 us (level)
  no operation moved by 1% of the time
where the time goes in v2:
time: 34.1 us; the launch traced here: 33.7 us
  Pallas kernels  31.7 us (93%)
  local copies, waits for them, and re-layouts  2.02 us (6%)
    pallas_call x1, Pallas kernels, local(): pl.pallas_call(make_kernel(nx, ny, size_x, size_y, half), out_shape=jax.S...  31.7 us
    unnamed x1, local copies, waits for them, and re-layouts  2.02 us

profile of v2, /device:TPU:12, one launch (start us, length us, event | category | flops | bytes accessed | tf_op | source)
XLA Modules:
  0.0 33.7 jit_solution(15990552641610188433)
XLA Ops:
  0.0 31.7 %smoothing.1 = f32[8,2,256,256]{3,2,1,0:T(8,128)S(1)} custom-call(f32[1024,256]{1,0:T(8,128)} %refs_0_.1, f32[8,2,256,256]{3,2,1,0:T(8,128)} %refs_1_.1), custom_call_target="tpu_custom_call" | custom-call | tf_op jit(solution)/shard_map/smoothing/pallas_call | solution.py:667
  31.7 2.0 %copy.4 = f32[8,2,256,256]{3,2,1,0:T(8,128)} copy(f32[8,2,256,256]{3,2,1,0:T(8,128)S(1)} %smoothing.1) | data formatting | bytes 8388608

commit v3 on v2

--- a/solution.py
+++ b/solution.py
@@ -335,9 +335,8 @@
                             accumulate(total, 0, value)
                     s[rb, c, r:r + CH, :] = total[0]
 
-        def normalise(rb):
-            each(z_sides, lambda side, target: z_arrival(side, target, rb).wait_recv())
-            for c in range(strips):
+        def normalise(rb, chosen):
+            for c in chosen:
                 for r in range(0, half, CH):
                     total = s[rb, c, r:r + CH, :]
                     if c == 0:
@@ -563,6 +562,7 @@
             smooth_first(rb, outer_strips)
             record(rb)
             each(z_sides, lambda side, target: z_copy(side, target, rb).start())
+            normalise(rb, inner_strips)
 
         @pl.loop(0, len(events))
         def _(k):
@@ -570,7 +570,8 @@
 
             @pl.when(rb >= 0)
             def _():
-                normalise(rb)
+                each(z_sides, lambda side, target: z_arrival(side, target, rb).wait_recv())
+                normalise(rb, outer_strips)
                 for side, at in ((0, 1), (1, nx - 1)):
                     @pl.when(rb == at)
                     def _():

time: 34.1 us -> 34 us (level)
  no operation moved by 1% of the time
where the time goes in v3:
time: 34 us; the launch traced here: 33.7 us
  Pallas kernels  31.7 us (93%)
  local copies, waits for them, and re-layouts  2.02 us (6%)
    pallas_call x1, Pallas kernels, local(): pl.pallas_call(make_kernel(nx, ny, size_x, size_y, half), out_shape=jax.S...  31.7 us
    unnamed x1, local copies, waits for them, and re-layouts  2.02 us

profile of v3, /device:TPU:12, one launch (start us, length us, event | category | flops | bytes accessed | tf_op | source)
XLA Modules:
  0.0 33.7 jit_solution(18211395762609185071)
XLA Ops:
  0.0 31.7 %smoothing.1 = f32[8,2,256,256]{3,2,1,0:T(8,128)S(1)} custom-call(f32[1024,256]{1,0:T(8,128)} %refs_0_.1, f32[8,2,256,256]{3,2,1,0:T(8,128)} %refs_1_.1), custom_call_target="tpu_custom_call" | custom-call | tf_op jit(solution)/shard_map/smoothing/pallas_call | solution.py:668
  31.7 2.0 %copy.4 = f32[8,2,256,256]{3,2,1,0:T(8,128)} copy(f32[8,2,256,256]{3,2,1,0:T(8,128)S(1)} %smoothing.1) | data formatting | bytes 8388608
